TPU v7x, 512 devices: a whole 4x4x16 slice. The times are simulated.
512 devices in a mesh: cuts: 128 (over z, x, core), stem: 4 (over y).
Axes of the slice: x: 4, y: 4, z: 16, core: 2. Of those that a mesh axis runs over, the one named last changes fastest.
Arguments:
- stem_tensor: bfloat16 [8, 64, 1024], P('stem'), may hold values from -6 to 6
- mid_tensors: bfloat16 [8192, 512, 128], P(('cuts', 'stem')), may hold values from -0.1875 to 0.1875
- right_tensors: bfloat16 [8, 8192, 64, 128], P(None, ('cuts', 'stem')), may hold values from -0.001953125 to 0.001953125
Outputs:
- amplitudes: float32 [8192], P('cuts')
All inputs are finite; a program needn't handle non-finite values.
Results may differ from a plain program's by a relative error of at most 0.0029.
Values may be sent and summed in bfloat16 or wider, within the bound.
A program may use at most 64 MiB of HBM per device.

v0:
```python
import jax
import jax.numpy as jnp
from jax import lax
from jax.sharding import PartitionSpec as P


def widen(tensor):
    half_width = tensor.shape[-1] // 2
    real_part = tensor[..., :half_width]
    imag_part = tensor[..., half_width:]
    upper_rows = jnp.concatenate([real_part, imag_part], axis=-1)
    lower_rows = jnp.concatenate([-imag_part, real_part], axis=-1)
    return jnp.concatenate([upper_rows, lower_rows], axis=-2)


def on_device(stem_tensor, mid_tensors, right_tensors):
    local_blocks, rows_a, width = stem_tensor.shape
    cols_b = right_tensors.shape[-1]
    widened = jnp.moveaxis(widen(mid_tensors), 0, 1).reshape(width, -1)
    fragment = lax.all_gather(stem_tensor, "stem", axis=0, tiled=True)
    flattened = fragment.reshape(-1, width)
    product = jnp.dot(flattened, widened, preferred_element_type=jnp.float32)
    first_step = product.astype(jnp.bfloat16).reshape(fragment.shape[0], rows_a, -1)
    right_wide = widen(right_tensors).reshape(first_step.shape[0], -1, cols_b)
    partial_sum = jnp.einsum(
        "iaq,iqb->ab", first_step, right_wide, preferred_element_type=jnp.float32
    ).reshape(-1)
    summed = lax.psum(partial_sum, ("cuts", "stem"))
    portion = partial_sum.shape[0] // lax.axis_size("cuts")
    return lax.dynamic_slice_in_dim(summed, lax.axis_index("cuts") * portion, portion)


def solution(mesh):
    return jax.shard_map(
        on_device,
        mesh=mesh,
        in_specs=(
            P("stem", None, None),
            P(("cuts", "stem"), None, None),
            P(None, ("cuts", "stem"), None, None),
        ),
        out_specs=P("cuts"),
        check_vma=False,
    )
```

profile of v0, /device:TPU:1, one launch (start us, length us, event | category | flops | bytes accessed | tf_op | source)
XLA Modules:
  0.0 163.8 jit_solution(10493150595197969950)
XLA Ops:
  6.5 0.0 all-gather.2.cloned.1.call-start
  6.5 0.7 all-gather.2.cloned.1.call-update
  7.3 2.9 %copy.9 = bf16[16,512,128]{1,2,0:T(8,128)(2,1)S(1)} copy(bf16[16,512,128]{2,1,0:T(8,128)(2,1)} %param.4) | data formatting | bytes 4194304 | tf_op args[1]
  10.1 0.1 slice_negate_fusion.1
  10.3 0.0 copy-start.1
  10.3 2.2 %maximum_maximum_fusion = bf16[16,1024,128]{1,2,0:T(8,128)(2,1)} fusion(bf16[16,512,64]{1,2,0:T(8,128)(2,1)S(1)} %get-tuple-element.8, bf16[16,512,64]{1,2,0:T(8,128)(2,1)S(1)} %get-tuple-element.7, bf16[16,512,128]{1,2,0:T(8,128)(2,1)S(1)} %copy.9), kind=kLoop, calls=%fused_computation | loop fusion | flops 12582912 | bytes 8388608 | tf_op jit(solution)/shard_map/concatenate | solution.py:13
  12.5 0.1 copy-done.1
  12.6 0.9 slice_negate_fusion
  13.5 3.5 %maximum_maximum_fusion.1 = bf16[8,16,128,128]{3,2,1,0:T(8,128)(2,1)} fusion(bf16[8,16,64,64]{3,2,1,0:T(8,128)(2,1)S(1)} %get-tuple-element.6, bf16[8,16,64,64]{3,2,1,0:T(8,128)(2,1)S(1)} %get-tuple-element.5, bf16[8,16,64,128]{3,2,1,0:T(8,128)(2,1)S(1)} %copy-done.1), kind=kLoop, calls=%fused_computation.1 | loop fusion | flops 12582912 | bytes 8388608 | tf_op jit(solution)/shard_map/concatenate | solution.py:13
  17.0 28.6 %all-gather.2.cloned.1.call-done = bf16[8,64,1024]{2,1,0:T(8,128)(2,1)} async-done(((bf16[2,64,1024]{2,1,0:T(8,128)(2,1)}), bf16[8,64,1024]{2,1,0:T(8,128)(2,1)}) %all-gather.2.cloned.1.call-update) | async-done | bytes 1048592 | tf_op jit(solution)/shard_map/all_gather | solution.py:20
  45.6 0.0 copy-start
  45.6 5.0 %convolution_convert_fusion = bf16[2048,512]{0,1:T(8,128)(2,1)S(1)} fusion(bf16[1024,2048]{0,1:T(8,128)(2,1)} %bitcast.18, bf16[512,1024]{1,0:T(8,128)(2,1)} %bitcast.19), kind=kOutput, calls=%fused_computation.2 | convolution fusion | flops 2148532224 | bytes 7340032 | tf_op jit(solution)/shard_map/dot_general | solution.py:22
  50.6 0.0 copy-done
  50.6 0.9 convolution_bitcast_fusion
  51.4 105.0 %psum.7 = f32[8192]{0:T(1024)S(1)} all-reduce(f32[8192]{0:T(1024)S(1)} %convolution_bitcast_fusion), channel_id=1, replica_groups=mesh['cuts'=128,'stem'=4] {'cuts','stem'}, use_global_device_ids=true, to_apply=%region_0.0 | all-reduce | flops 8192 | bytes 65536 | tf_op jit(solution)/shard_map/psum | solution.py:28
  156.4 0.6 dynamic_slice.3
Async XLA Ops:
  6.5 39.0 %all-gather.2.cloned.1.call-start = ((), (), s32[]{:S(2)}) async-start(), calls=%async_computation | async-start | bytes 1310720 | tf_op jit(solution)/shard_map/all_gather | solution.py:20
  10.3 2.3 %copy-start.1 = (bf16[8,16,64,128]{3,2,1,0:T(8,128)(2,1)S(1)}, bf16[8,16,64,128]{3,2,1,0:T(8,128)(2,1)}, u32[]{:S(2)}) copy-start(bf16[8,16,64,128]{3,2,1,0:T(8,128)(2,1)} %param.5) | copy-start | bytes 6291460
  45.6 5.0 %copy-start = (bf16[8,16,128,128]{3,2,1,0:T(8,128)(2,1)S(1)}, bf16[8,16,128,128]{3,2,1,0:T(8,128)(2,1)}, u32[]{:S(2)}) copy-start(bf16[8,16,128,128]{3,2,1,0:T(8,128)(2,1)} %maximum_maximum_fusion.1) | copy-start | bytes 12582916
Sparse Core Ops, SparseCore 0:
  9.5 36.0 all-gather.1
where the time goes:
time: 164 us
  blocking collectives  105 us (64%)
  waiting for transfers between devices  29.3 us (18%)
  between operations  13.4 us (8%)
  other arithmetic  6.78 us (4%)
  matrix products  5.86 us (4%)
  local copies, waits for them, and re-layouts  3.52 us (2%)
    psum x1, blocking collectives, on_device(): summed = lax.psum(partial_sum, ('cuts', 'stem'))  105 us
    all_gather x1, waiting for transfers between devices, on_device(): fragment = lax.all_gather(stem_tensor, 'stem', axis=0, tiled=True)  28.6 us
    concatenate x2, other arithmetic, widen(): return jnp.concatenate([upper_rows, lower_rows], axis=-2)  5.77 us
    dot_general x1, matrix products, on_device(): product = jnp.dot(flattened, widened, preferred_element_type=jnp.float32)  5.01 us
  transfers between devices with their start and end apart: 1, of which 1 were waited for; matrix products, arithmetic and copies ran while one was open for 6% of the time, Pallas kernels for 0%

commit v1 on v0

--- a/solution.py
+++ b/solution.py
@@ -17,7 +17,28 @@
     local_blocks, rows_a, width = stem_tensor.shape
     cols_b = right_tensors.shape[-1]
     widened = jnp.moveaxis(widen(mid_tensors), 0, 1).reshape(width, -1)
-    fragment = lax.all_gather(stem_tensor, "stem", axis=0, tiled=True)
+
+    def store_islands(point):
+        now, plain, wide_out = (lax.axis_size("stem"), lax.axis_index("stem"), point.shape[0])
+        views = tuple(((j, (j + 1) % now) for j in range(now)))
+        pool = tuple(((j, (j - 1) % now) for j in range(now)))
+        latest = jnp.zeros((*point.shape[:0], now * wide_out, *point.shape[1:]), point.dtype)
+        latest = lax.dynamic_update_slice_in_dim(latest, point, plain * wide_out, axis=0)
+        aux = vec_out = point
+        z2 = now // 2
+        for num in range(1, z2 + 1):
+            aux = lax.ppermute(aux, "stem", views)
+            latest = lax.dynamic_update_slice_in_dim(
+                latest, aux, (plain - num) % now * wide_out, axis=0
+            )
+            if num < now - z2:
+                vec_out = lax.ppermute(vec_out, "stem", pool)
+                latest = lax.dynamic_update_slice_in_dim(
+                    latest, vec_out, (plain + num) % now * wide_out, axis=0
+                )
+        return latest
+
+    fragment = store_islands(stem_tensor)
     flattened = fragment.reshape(-1, width)
     product = jnp.dot(flattened, widened, preferred_element_type=jnp.float32)
     first_step = product.astype(jnp.bfloat16).reshape(fragment.shape[0], rows_a, -1)

time: 164 us -> 146 us (0.89)
  waiting for transfers between devices: 29.3 us -> 6.1 us
  between operations: 13.4 us -> 0.2 us
  starting transfers between devices: 0.01 us -> 9.43 us
  blocking collectives: 105 us -> 111 us
  local copies, waits for them, and re-layouts: 3.52 us -> 5.44 us
    all_gather x1 -> x0, waiting for transfers between devices: 28.6 us -> none  [on_device(): fragment = lax.all_gather(stem_tensor, 'stem', axis=0, tiled=True)]
    ppermute x0 -> x3, starting transfers between devices: none -> 9.43 us  [the longest x1 5.59 us: store_islands(): vec_out = lax.ppermute(vec_out, 'stem', pool)]
    ppermute x0 -> x3, waiting for transfers between devices: none -> 6.1 us  [the longest x2 6.09 us: store_islands(): aux = lax.ppermute(aux, 'stem', views)]
    psum x1, blocking collectives: 105 us -> 111 us  [on_device(): summed = lax.psum(partial_sum, ('cuts', 'stem'))]
    unnamed x5 -> x9, local copies, waits for them, and re-layouts: 2.94 us -> 4.65 us
  transfers between devices with their start and end apart: 1 -> 3, of which waited for: 1 -> 1; matrix products, arithmetic and copies ran while one was open for 6% -> 9% of each run, Pallas kernels for 0% -> 0%
where the time goes in v1:
time: 146 us
  blocking collectives  111 us (76%)
  starting transfers between devices  9.43 us (6%)
  other arithmetic  8.32 us (6%)
  waiting for transfers between devices  6.1 us (4%)
  matrix products  5.56 us (4%)
  local copies, waits for them, and re-layouts  5.44 us (4%)
    psum x1, blocking collectives, on_device(): summed = lax.psum(partial_sum, ('cuts', 'stem'))  111 us
    ppermute x2, waiting for transfers between devices, store_islands(): aux = lax.ppermute(aux, 'stem', views)  6.09 us
    concatenate x2, other arithmetic, widen(): return jnp.concatenate([upper_rows, lower_rows], axis=-2)  5.76 us
    ppermute x1, starting transfers between devices, store_islands(): vec_out = lax.ppermute(vec_out, 'stem', pool)  5.59 us
    dot_general x1, matrix products, on_device(): product = jnp.dot(flattened, widened, preferred_element_type=jnp.float32)  4.7 us
    unnamed x9, local copies, waits for them, and re-layouts  4.65 us
    ppermute x2, starting transfers between devices, store_islands(): aux = lax.ppermute(aux, 'stem', views)  3.84 us
  transfers between devices with their start and end apart: 3, of which 1 were waited for; matrix products, arithmetic and copies ran while one was open for 9% of the time, Pallas kernels for 0%

profile of v1, /device:TPU:1, one launch (start us, length us, event | category | flops | bytes accessed | tf_op | source)
XLA Modules:
  0.0 146.0 jit_solution(11486843459742263428)
XLA Ops:
  0.0 0.0 copy-start.1
  0.0 5.6 %collective-permute-start.1 = (bf16[2,64,1024]{2,1,0:T(8,128)(2,1)}, bf16[2,64,1024]{2,1,0:T(8,128)(2,1)S(1)}, u32[]{:S(2)}, u32[]{:S(2)}) collective-permute-start(bf16[2,64,1024]{2,1,0:T(8,128)(2,1)} %param.3), channel_id=1, source_target_pairs={{0,3},{1,0},{2,1},{3,2},{4,7},{5,4},{6,5},{7,6},{8,11},{9,8},{10,9... | collective-permute-start | bytes 786440 | tf_op jit(solution)/shard_map/ppermute | solution.py:35
  5.6 1.9 %collective-permute-start = (bf16[2,64,1024]{2,1,0:T(8,128)(2,1)}, bf16[2,64,1024]{2,1,0:T(8,128)(2,1)S(1)}, u32[]{:S(2)}, u32[]{:S(2)}) collective-permute-start(bf16[2,64,1024]{2,1,0:T(8,128)(2,1)} %param.3), channel_id=1, source_target_pairs={{0,1},{1,2},{2,3},{3,0},{4,5},{5,6},{6,7},{7,4},{8,9},{9,10},{10,1... | collective-permute-start | bytes 786440 | tf_op jit(solution)/shard_map/ppermute | solution.py:30
  7.5 3.9 %copy.6 = bf16[16,512,128]{1,2,0:T(8,128)(2,1)} copy(bf16[16,512,128]{2,1,0:T(8,128)(2,1)} %param.4) | data formatting | bytes 4194304 | tf_op args[1]
  11.5 1.7 %slice_negate_fusion.1 = (bf16[16,512,64]{1,2,0:T(8,128)(2,1)S(1)}, bf16[16,512,64]{1,2,0:T(8,128)(2,1)S(1)}) fusion(bf16[16,512,128]{1,2,0:T(8,128)(2,1)} %copy.6), kind=kLoop, calls=%fused_computation.5 | loop fusion | flops 524288 | bytes 4194304 | tf_op jit(solution)/shard_map/neg | solution.py:12
  13.1 0.0 copy-done.1
  13.2 0.0 copy-start.2
  13.2 0.9 slice_negate_fusion
  14.0 0.7 copy-done.2
  14.7 2.2 %maximum_maximum_fusion = bf16[16,1024,128]{1,2,0:T(8,128)(2,1)} fusion(bf16[16,512,64]{1,2,0:T(8,128)(2,1)S(1)} %get-tuple-element.8, bf16[16,512,64]{1,2,0:T(8,128)(2,1)S(1)} %get-tuple-element.7, bf16[16,512,128]{1,2,0:T(8,128)(2,1)S(1)} %copy-done.2), kind=kLoop, calls=%fused_computation | loop fusion | flops 12582912 | bytes 8388608 | tf_op jit(solution)/shard_map/concatenate | solution.py:13
  17.0 0.0 copy-start.3
  17.0 3.6 %maximum_maximum_fusion.1 = bf16[8,16,128,128]{3,2,1,0:T(8,128)(2,1)} fusion(bf16[8,16,64,64]{3,2,1,0:T(8,128)(2,1)S(1)} %get-tuple-element.6, bf16[8,16,64,64]{3,2,1,0:T(8,128)(2,1)S(1)} %get-tuple-element.5, bf16[8,16,64,128]{3,2,1,0:T(8,128)(2,1)S(1)} %copy-done.1), kind=kLoop, calls=%fused_computation.1 | loop fusion | flops 12582912 | bytes 8388608 | tf_op jit(solution)/shard_map/concatenate | solution.py:13
  20.5 0.0 collective-permute-done
  20.5 1.9 %collective-permute-start.2 = (bf16[2,64,1024]{2,1,0:T(8,128)(2,1)S(1)}, bf16[2,64,1024]{2,1,0:T(8,128)(2,1)S(1)}, u32[]{:S(2)}, u32[]{:S(2)}) collective-permute-start(bf16[2,64,1024]{2,1,0:T(8,128)(2,1)S(1)} %collective-permute-done), channel_id=1, source_target_pairs={{0,1},{1,2},{2,3},{3,0},{4,5},{5,6},{6,7},{7,4},{8,9},{9,10},{10,1... | collective-permute-start | bytes 786440 | tf_op jit(solution)/shard_map/ppermute | solution.py:30
  22.4 0.1 broadcast_in_dim.3
  22.6 0.0 copy-done.3
  22.7 0.0 collective-permute-done.1
  22.7 6.1 %collective-permute-done.2 = bf16[2,64,1024]{2,1,0:T(8,128)(2,1)S(1)} collective-permute-done((bf16[2,64,1024]{2,1,0:T(8,128)(2,1)S(1)}, bf16[2,64,1024]{2,1,0:T(8,128)(2,1)S(1)}, u32[]{:S(2)}, u32[]{:S(2)}) %collective-permute-start.2) | collective-permute-done | bytes 262176 | tf_op jit(solution)/shard_map/ppermute | solution.py:30
  28.9 0.0 copy-start
  28.9 4.7 %convolution_convert_fusion = bf16[512,2048]{1,0:T(8,128)(2,1)S(1)} fusion(bf16[512,1024]{1,0:T(8,128)(2,1)S(1)} %bitcast.17, bf16[1024,2048]{0,1:T(8,128)(2,1)} %bitcast.16), kind=kOutput, calls=%fused_computation.2 | convolution fusion | flops 2148532224 | bytes 7340032 | tf_op jit(solution)/shard_map/dot_general | solution.py:43
  33.6 0.0 copy-done
  33.6 0.9 convolution_bitcast_fusion
  34.5 111.0 %psum.7 = f32[8192]{0:T(1024)S(1)} all-reduce(f32[8192]{0:T(1024)S(1)} %convolution_bitcast_fusion), channel_id=1, replica_groups=mesh['cuts'=128,'stem'=4] {'cuts','stem'}, use_global_device_ids=true, to_apply=%region_0.1 | all-reduce | flops 8192 | bytes 65536 | tf_op jit(solution)/shard_map/psum | solution.py:49
  145.4 0.6 dynamic_slice.3
  (4 shorter events, 0.1 us)
Async XLA Ops:
  0.0 13.1 %copy-start.1 = (bf16[8,16,64,128]{3,2,1,0:T(8,128)(2,1)S(1)}, bf16[8,16,64,128]{3,2,1,0:T(8,128)(2,1)}, u32[]{:S(2)}) copy-start(bf16[8,16,64,128]{3,2,1,0:T(8,128)(2,1)} %param.5) | copy-start | bytes 6291460
  0.0 22.7 %collective-permute-start.1 = (bf16[2,64,1024]{2,1,0:T(8,128)(2,1)}, bf16[2,64,1024]{2,1,0:T(8,128)(2,1)S(1)}, u32[]{:S(2)}, u32[]{:S(2)}) collective-permute-start(bf16[2,64,1024]{2,1,0:T(8,128)(2,1)} %param.3), channel_id=1, source_target_pairs={{0,3},{1,0},{2,1},{3,2},{4,7},{5,4},{6,5},{7,6},{8,11},{9,8},{10,9... | collective-permute-start | bytes 786440 | tf_op jit(solution)/shard_map/ppermute | solution.py:35
  5.6 14.9 %collective-permute-start = (bf16[2,64,1024]{2,1,0:T(8,128)(2,1)}, bf16[2,64,1024]{2,1,0:T(8,128)(2,1)S(1)}, u32[]{:S(2)}, u32[]{:S(2)}) collective-permute-start(bf16[2,64,1024]{2,1,0:T(8,128)(2,1)} %param.3), channel_id=1, source_target_pairs={{0,1},{1,2},{2,3},{3,0},{4,5},{5,6},{6,7},{7,4},{8,9},{9,10},{10,1... | collective-permute-start | bytes 786440 | tf_op jit(solution)/shard_map/ppermute | solution.py:30
  13.2 1.6 %copy-start.2 = (bf16[16,512,128]{1,2,0:T(8,128)(2,1)S(1)}, bf16[16,512,128]{1,2,0:T(8,128)(2,1)}, u32[]{:S(2)}) copy-start(bf16[16,512,128]{1,2,0:T(8,128)(2,1)} %copy.6) | copy-start | bytes 6291460
  17.0 5.6 %copy-start.3 = (bf16[2,64,1024]{2,1,0:T(8,128)(2,1)S(1)}, bf16[2,64,1024]{2,1,0:T(8,128)(2,1)}, u32[]{:S(2)}) copy-start(bf16[2,64,1024]{2,1,0:T(8,128)(2,1)} %param.3) | copy-start | bytes 786436
  20.5 8.3 %collective-permute-start.2 = (bf16[2,64,1024]{2,1,0:T(8,128)(2,1)S(1)}, bf16[2,64,1024]{2,1,0:T(8,128)(2,1)S(1)}, u32[]{:S(2)}, u32[]{:S(2)}) collective-permute-start(bf16[2,64,1024]{2,1,0:T(8,128)(2,1)S(1)} %collective-permute-done), channel_id=1, source_target_pairs={{0,1},{1,2},{2,3},{3,0},{4,5},{5,6},{6,7},{7,4},{8,9},{9,10},{10,1... | collective-permute-start | bytes 786440 | tf_op jit(solution)/shard_map/ppermute | solution.py:30
  28.9 4.7 %copy-start = (bf16[8,16,128,128]{3,2,1,0:T(8,128)(2,1)S(1)}, bf16[8,16,128,128]{3,2,1,0:T(8,128)(2,1)}, u32[]{:S(2)}) copy-start(bf16[8,16,128,128]{3,2,1,0:T(8,128)(2,1)} %maximum_maximum_fusion.1) | copy-start | bytes 12582916
